TPU v7x, 32 devices: a whole 2x2x4 slice. The times are simulated.
32 devices in a mesh: curve: 8 (over z, x), sub: 4 (over y, core).
Axes of the slice: x: 2, y: 2, z: 4, core: 2. Of those that a mesh axis runs over, the one named last changes fastest.
Arguments:
- load: float32 [3, 32, 64, 128], P(None, 'sub', 'curve'), may hold values from -6 to 6
- plastic: float32 [32, 64, 128], P('sub', 'curve'), may hold values from 0 to 0.95, as said below
- tile_material: int32 [4, 8, 16], P('sub', 'curve'), may hold values from 0 to 4
- moduli: float32 [4], replicated, may hold values from 0.5 to 4
- k_vol: float32 [24, 24], replicated
- k_dev: float32 [24, 24], replicated
Outputs:
- solution: float32 [3, 32, 64, 128], P(None, 'sub', 'curve')
- residual: float32 [3, 32, 64, 128], P(None, 'sub', 'curve')
Inputs may be any that keep to these rules, and one draw needn't show every extreme that they name: `plastic`: zero for voxels that have not yielded, else the share lost.
All inputs are finite; a program needn't handle non-finite values.
Results may differ from a plain program's by a relative error of at most 0.0003.
Values sent between devices are 32-bit elements; how exact they have to be, the bound alone decides.
No kernel may reach another device: no remote copies, remote signals or barrier semaphores. Data moves between devices by JAX's collectives and lax.ppermute only.
A program may use at most 64 MiB of HBM per device.

v0:
```python
import jax
import jax.numpy as jnp
from jax import lax
from jax.sharding import PartitionSpec as P

TILE = 8
MATERIALS = 4
ITERS = 3
ground_spring = 0.5


def shifted(value, axis, by):
    count = lax.axis_size(axis)
    pairs = [(i, i + by) for i in range(count) if 0 <= i + by < count]
    return lax.ppermute(value, axis, pairs)


def padded(block, sides, width):
    for axis, dim in sides:
        count = lax.axis_size(axis)
        forward = [(i, i + 1) for i in range(count - 1)]
        backward = [(target, source) for source, target in forward]
        low = lax.ppermute(
            lax.slice_in_dim(block, block.shape[dim] - width, None, axis=dim), axis, forward
        )
        high = lax.ppermute(lax.slice_in_dim(block, 0, width, axis=dim), axis, backward)
        block = jnp.concatenate([low, block, high], axis=dim)
    return block


def voxel_coefficients(tile_material, moduli, plastic):
    one_hot = (tile_material[..., None] == jnp.arange(1, MATERIALS + 1, dtype=jnp.int32)).astype(
        jnp.float32
    )
    tile_modulus = jnp.sum(one_hot * moduli, axis=-1)
    voxel_modulus = jnp.repeat(jnp.repeat(jnp.repeat(tile_modulus, TILE, 0), TILE, 1), TILE, 2)
    return jnp.stack([voxel_modulus, voxel_modulus * (1.0 - plastic)])


def shift_second(values, along_y):
    if along_y == 0:
        return values
    zeros_col = jnp.zeros(values.shape[:-1] + (1,), values.dtype)
    return jnp.concatenate([zeros_col, values[..., :-1]], axis=-1)


def keep_mask(extended, first_x, first_z):
    size_x = extended.shape[1] - 1
    size_z = extended.shape[2] - 1
    size_y = extended.shape[3]
    occupied = (extended[0] > 0).astype(jnp.float32)
    active = jnp.zeros((size_x, size_z, size_y), jnp.float32)
    for along_x in (0, 1):
        for along_z in (0, 1):
            for along_y in (0, 1):
                contrib = occupied[
                    1 - along_x : 1 - along_x + size_x, 1 - along_z : 1 - along_z + size_z, :
                ]
                active = jnp.maximum(active, shift_second(contrib, along_y))
    index_x = first_x + jnp.arange(size_x, dtype=jnp.int32)
    index_z = first_z + jnp.arange(size_z, dtype=jnp.int32)
    index_y = jnp.arange(size_y, dtype=jnp.int32)
    free = (
        (index_x > 0)[:, None, None] & (index_z > 0)[None, :, None] & (index_y > 0)[None, None, :]
    )
    return active * free.astype(jnp.float32)


def node_forces(bordered, extended, k_vol, k_dev):
    size_x = extended.shape[1] - 1
    size_z = extended.shape[2] - 1
    size_y = extended.shape[3]
    lower = jnp.moveaxis(bordered[:, 0 : size_x + 1], 1, 0)
    upper = jnp.moveaxis(bordered[:, 1 : size_x + 2], 1, 0)
    layer_coef = jnp.moveaxis(extended, 1, 0)
    k_both = jnp.concatenate([k_vol, k_dev], axis=1)

    def assemble(forces, along_x):
        summed = jnp.zeros((3, size_z, size_y), jnp.float32)
        for along_z in (0, 1):
            for along_y in (0, 1):
                contrib = forces[along_x * 4 + along_z * 2 + along_y][
                    :, 1 - along_z : 1 - along_z + size_z, :
                ]
                summed = summed + shift_second(contrib, along_y)
        return summed

    def layer(carried, layer_item):
        lower_nodes, upper_nodes, coef_layer = layer_item
        corners = []
        for source in (lower_nodes, upper_nodes):
            for along_z in (0, 1):
                block = source[:, along_z : along_z + size_z + 1, :]
                corners.append(block)
                zeros_col = jnp.zeros((3, size_z + 1, 1), jnp.float32)
                corners.append(jnp.concatenate([block[:, :, 1:], zeros_col], axis=2))
        element = jnp.concatenate(corners, 0).reshape(24, (size_z + 1) * size_y)
        vol_scale = coef_layer[0].reshape(1, -1)
        dev_scale = coef_layer[1].reshape(1, -1)
        scaled = jnp.concatenate([vol_scale * element, dev_scale * element], axis=0)
        forces = jnp.dot(
            k_both, scaled, precision=lax.Precision.HIGHEST, preferred_element_type=jnp.float32
        )
        forces = forces.reshape(8, 3, size_z + 1, size_y)
        return (assemble(forces, 1), carried + assemble(forces, 0))

    start = jnp.zeros((3, size_z, size_y), jnp.float32)
    _, emitted = lax.scan(layer, start, (lower, upper, layer_coef))
    return jnp.moveaxis(emitted[1:], 0, 1)


def inner_sums(residual, image):
    return lax.psum((jnp.sum(residual * residual), jnp.sum(residual * image)), ("curve", "sub"))


def local(load, plastic, tile_material, moduli, k_vol, k_dev):
    coefficients = voxel_coefficients(tile_material, moduli, plastic)
    below_x = shifted(coefficients[:, -1:], "sub", 1)
    extended = jnp.concatenate([below_x, coefficients], axis=1)
    below_z = shifted(extended[:, :, -1:], "curve", 1)
    extended = jnp.concatenate([below_z, extended], axis=2)
    first_x = lax.axis_index("sub") * coefficients.shape[1]
    first_z = lax.axis_index("curve") * coefficients.shape[2]
    keep = keep_mask(extended, first_x, first_z)

    def operate(field_vals):
        bordered = padded(field_vals, (("curve", 2), ("sub", 1)), 1)
        return keep * (node_forces(bordered, extended, k_vol, k_dev) + ground_spring * field_vals)

    residual = keep * load
    solution = jnp.zeros_like(residual)
    image = operate(residual)
    norm_now, curvature = inner_sums(residual, image)
    step_size = norm_now / curvature
    direction = residual
    carried = image
    for iteration in range(ITERS):
        solution = solution + step_size * direction
        residual = residual - step_size * carried
        if iteration + 1 < ITERS:
            image = operate(residual)
            norm_next, curvature = inner_sums(residual, image)
            next_ratio = norm_next / norm_now
            step_size = norm_next / (curvature - next_ratio * norm_next / step_size)
            direction = residual + next_ratio * direction
            carried = image + next_ratio * carried
            norm_now = norm_next
    return (solution, residual)


def solution(mesh):
    in_specs = (
        P(None, "sub", "curve", None),
        P("sub", "curve", None),
        P("sub", "curve", None),
        P(),
        P(),
        P(),
    )
    out_specs = (P(None, "sub", "curve", None), P(None, "sub", "curve", None))
    return jax.shard_map(local, mesh=mesh, in_specs=in_specs, out_specs=out_specs, check_vma=False)
```

profile of v0, /device:TPU:0, one launch (start us, length us, event | category | flops | bytes accessed | tf_op | source)
XLA Modules:
  0.0 229.4 jit_solution(9882357935380456547)
XLA Ops:
  0.7 0.6 copy-done.3
  1.5 0.1 broadcast_in_dim.35
  1.6 0.8 multiply_bitcast_fusion
  2.4 2.4 %collective-permute-start = (f32[2,1,8,128]{3,2,0,1:T(8,128)S(1)}, f32[2,1,8,128]{3,2,0,1:T(8,128)S(1)}, u32[]{:S(2)}, u32[]{:S(2)}) collective-permute-start(f32[2,1,8,128]{3,2,0,1:T(8,128)S(1)} %pad_maximum_fusion.12), channel_id=1, source_target_pairs={{0,1},{1,2},{2,3},{4,5},{5,6},{6,7},{8,9},{9,10},{10,11},{12,13},{... | collective-permute-start | bytes 24584 | tf_op jit(solution)/shard_map/ppermute | solution.py:15
  4.8 0.7 collective-permute-done
  5.6 4.2 %collective-permute-start.1 = (f32[2,9,1,128]{3,2,0,1:T(1,128)S(1)}, f32[2,9,1,128]{3,2,0,1:T(1,128)S(1)}, u32[]{:S(2)}, u32[]{:S(2)}) collective-permute-start(f32[2,9,1,128]{3,2,0,1:T(1,128)S(1)} %pad_maximum_fusion.10), channel_id=1, source_target_pairs={{0,4},{4,8},{8,12},{12,16},{16,20},{20,24},{24,28},{1,5},{5,9},{9,... | collective-permute-start | bytes 27656 | tf_op jit(solution)/shard_map/ppermute | solution.py:15
  9.8 1.3 collective-permute-done.1
  11.2 0.1 fusion.31
  11.4 0.8 copy-done
  12.2 4.2 %collective-permute-start.2 = (f32[3,8,1,128]{3,2,1,0:T(1,128)S(1)}, f32[3,8,1,128]{3,2,1,0:T(1,128)S(1)}, u32[]{:S(2)}, u32[]{:S(2)}) collective-permute-start(f32[3,8,1,128]{3,2,1,0:T(1,128)S(1)} %get-tuple-element.379), channel_id=1, source_target_pairs={{0,4},{4,8},{8,12},{12,16},{16,20},{20,24},{24,28},{1,5},{5,9},{9,... | collective-permute-start | bytes 36872 | tf_op jit(solution)/shard_map/ppermute | solution.py:23
  16.4 1.3 collective-permute-start.3
  17.7 4.6 %collective-permute-done.3 = f32[3,8,1,128]{3,2,1,0:T(1,128)S(1)} collective-permute-done((f32[3,8,1,128]{3,2,1,0:T(1,128)S(1)}, f32[3,8,1,128]{3,2,1,0:T(1,128)S(1)}, u32[]{:S(2)}, u32[]{:S(2)}) %collective-permute-start.3) | collective-permute-done | bytes 12320 | tf_op jit(solution)/shard_map/ppermute | solution.py:26
  22.4 1.4 collective-permute-start.4
  23.8 1.3 collective-permute-start.5
  25.2 5.8 %collective-permute-done.5 = f32[3,1,10,128]{3,2,1,0:T(8,128)S(1)} collective-permute-done((f32[3,1,10,128]{3,2,1,0:T(8,128)S(1)}, f32[3,1,10,128]{3,2,1,0:T(8,128)S(1)}, u32[]{:S(2)}, u32[]{:S(2)}) %collective-permute-start.5) | collective-permute-done | bytes 15392 | tf_op jit(solution)/shard_map/ppermute | solution.py:26
  31.0 9.3 %while.39 = (s32[]{:T(128)}, f32[3,8,128]{2,1,0:T(8,128)S(1)}, f32[9,3,8,128]{3,2,0,1:T(8,128)S(1)}, f32[9,2,9,128]{3,2,1,0:T(8,128)S(1)}, f32[9,3,10,128]{3,2,0...) while((s32[]{:T(128)}, f32[3,8,128]{2,1,0:T(8,128)S(1)}, ...), condition=%wide.region_4.5_spmd.clone, body=%wide.region_3.4_spmd.clone.sunk | while | flops 16060420 | bytes 1924459 | solution.py:108
  31.4 0.3 convolution_bitcast_fusion.6
  32.4 0.3 convolution_bitcast_fusion.6
  33.5 0.3 convolution_bitcast_fusion.6
  34.5 0.3 convolution_bitcast_fusion.6
  35.5 0.3 convolution_bitcast_fusion.6
  36.5 0.3 convolution_bitcast_fusion.6
  37.6 0.3 convolution_bitcast_fusion.6
  38.6 0.3 convolution_bitcast_fusion.6
  39.6 0.3 convolution_bitcast_fusion.6
  40.3 0.6 multiply_reduce_fusion.4
  40.9 43.1 %all-reduce.30 = (f32[]{:T(128)}, f32[]{:T(128)}) all-reduce(f32[]{:T(128)} %get-tuple-element.256, f32[]{:T(128)} %get-tuple-element.255), channel_id=1, replica_groups=mesh['curve'=8,'sub'=4] {'curve','sub'}, use_global_device_ids=true, to_apply=%region_2.3 | all-reduce | flops 2 | bytes 16 | tf_op jit(solution)/shard_map/psum | solution.py:113
  85.5 4.2 %collective-permute-start.6 = (f32[3,8,1,128]{3,2,1,0:T(1,128)S(1)}, f32[3,8,1,128]{3,2,1,0:T(1,128)S(1)}, u32[]{:S(2)}, u32[]{:S(2)}) collective-permute-start(f32[3,8,1,128]{3,2,1,0:T(1,128)S(1)} %get-tuple-element.377), channel_id=1, source_target_pairs={{0,4},{4,8},{8,12},{12,16},{16,20},{20,24},{24,28},{1,5},{5,9},{9,... | collective-permute-start | bytes 36872 | tf_op jit(solution)/shard_map/ppermute | solution.py:23
  89.6 1.3 collective-permute-start.7
  91.0 4.2 %collective-permute-done.7 = f32[3,8,1,128]{3,2,1,0:T(1,128)S(1)} collective-permute-done((f32[3,8,1,128]{3,2,1,0:T(1,128)S(1)}, f32[3,8,1,128]{3,2,1,0:T(1,128)S(1)}, u32[]{:S(2)}, u32[]{:S(2)}) %collective-permute-start.7) | collective-permute-done | bytes 12320 | tf_op jit(solution)/shard_map/ppermute | solution.py:26
  95.2 1.3 collective-permute-start.8
  96.5 1.3 collective-permute-start.9
  97.9 2.2 collective-permute-done.9
  100.2 9.3 %while.40 = (s32[]{:T(128)}, f32[3,8,128]{2,1,0:T(8,128)S(1)}, f32[9,3,8,128]{3,2,0,1:T(8,128)S(1)}, f32[9,2,9,128]{3,2,1,0:T(8,128)S(1)}, f32[9,3,10,128]{3,2,0...) while((s32[]{:T(128)}, f32[3,8,128]{2,1,0:T(8,128)S(1)}, ...), condition=%wide.region_10.11_spmd.clone, body=%wide.region_9.10_spmd.clone.sunk | while | flops 16060420 | bytes 1924459 | solution.py:108
  100.5 0.3 convolution_bitcast_fusion.7
  101.6 0.3 convolution_bitcast_fusion.7
  102.6 0.3 convolution_bitcast_fusion.7
  103.6 0.3 convolution_bitcast_fusion.7
  104.6 0.3 convolution_bitcast_fusion.7
  105.7 0.3 convolution_bitcast_fusion.7
  106.7 0.3 convolution_bitcast_fusion.7
  107.7 0.3 convolution_bitcast_fusion.7
  108.7 0.3 convolution_bitcast_fusion.7
  109.4 0.7 multiply_reduce_fusion.2
  110.2 42.8 %all-reduce.29 = (f32[]{:T(128)}, f32[]{:T(128)}) all-reduce(f32[]{:T(128)} %get-tuple-element.254, f32[]{:T(128)} %get-tuple-element.253), channel_id=1, replica_groups=mesh['curve'=8,'sub'=4] {'curve','sub'}, use_global_device_ids=true, to_apply=%region_8.9 | all-reduce | flops 2 | bytes 16 | tf_op jit(solution)/shard_map/psum | solution.py:113
  157.4 4.2 %collective-permute-start.10 = (f32[3,8,1,128]{3,2,1,0:T(1,128)S(1)}, f32[3,8,1,128]{3,2,1,0:T(1,128)S(1)}, u32[]{:S(2)}, u32[]{:S(2)}) collective-permute-start(f32[3,8,1,128]{3,2,1,0:T(1,128)S(1)} %get-tuple-element.375), channel_id=1, source_target_pairs={{0,4},{4,8},{8,12},{12,16},{16,20},{20,24},{24,28},{1,5},{5,9},{9,... | collective-permute-start | bytes 36872 | tf_op jit(solution)/shard_map/ppermute | solution.py:23
  161.6 1.3 collective-permute-start.11
  163.0 4.2 %collective-permute-done.11 = f32[3,8,1,128]{3,2,1,0:T(1,128)S(1)} collective-permute-done((f32[3,8,1,128]{3,2,1,0:T(1,128)S(1)}, f32[3,8,1,128]{3,2,1,0:T(1,128)S(1)}, u32[]{:S(2)}, u32[]{:S(2)}) %collective-permute-start.11) | collective-permute-done | bytes 12320 | tf_op jit(solution)/shard_map/ppermute | solution.py:26
  167.2 1.3 collective-permute-start.12
  168.5 1.3 collective-permute-start.13
  169.8 2.3 collective-permute-done.13
  172.2 9.3 %while.41 = (s32[]{:T(128)}, f32[3,8,128]{2,1,0:T(8,128)S(1)}, f32[9,3,8,128]{3,2,0,1:T(8,128)S(1)}, f32[9,2,9,128]{3,2,1,0:T(8,128)S(1)}, f32[9,3,10,128]{3,2,0...) while((s32[]{:T(128)}, f32[3,8,128]{2,1,0:T(8,128)S(1)}, ...), condition=%wide.region_16.17_spmd.clone, body=%wide.region_15.16_spmd.clone.sunk | while | flops 16060420 | bytes 1924459 | solution.py:108
  172.5 0.3 convolution_bitcast_fusion.8
  173.6 0.3 convolution_bitcast_fusion.8
  174.6 0.3 convolution_bitcast_fusion.8
  175.6 0.3 convolution_bitcast_fusion.8
  176.6 0.3 convolution_bitcast_fusion.8
  177.7 0.3 convolution_bitcast_fusion.8
  178.7 0.3 convolution_bitcast_fusion.8
  179.7 0.3 convolution_bitcast_fusion.8
  180.8 0.3 convolution_bitcast_fusion.8
  181.4 0.6 multiply_reduce_fusion
  182.1 42.8 %all-reduce.28 = (f32[]{:T(128)}, f32[]{:T(128)}) all-reduce(f32[]{:T(128)} %get-tuple-element.252, f32[]{:T(128)} %get-tuple-element.251), channel_id=1, replica_groups=mesh['curve'=8,'sub'=4] {'curve','sub'}, use_global_device_ids=true, to_apply=%region_14.15 | all-reduce | flops 2 | bytes 16 | tf_op jit(solution)/shard_map/psum | solution.py:113
  228.7 0.7 multiply_subtract_fusion
  (801 shorter events, 17.0 us)
Async XLA Ops:
  0.6 0.7 copy-start.3
  0.7 0.7 copy-start.4
  2.4 3.2 %collective-permute-start = (f32[2,1,8,128]{3,2,0,1:T(8,128)S(1)}, f32[2,1,8,128]{3,2,0,1:T(8,128)S(1)}, u32[]{:S(2)}, u32[]{:S(2)}) collective-permute-start(f32[2,1,8,128]{3,2,0,1:T(8,128)S(1)} %pad_maximum_fusion.12), channel_id=1, source_target_pairs={{0,1},{1,2},{2,3},{4,5},{5,6},{6,7},{8,9},{9,10},{10,11},{12,13},{... | collective-permute-start | bytes 24584 | tf_op jit(solution)/shard_map/ppermute | solution.py:15
  5.6 5.6 %collective-permute-start.1 = (f32[2,9,1,128]{3,2,0,1:T(1,128)S(1)}, f32[2,9,1,128]{3,2,0,1:T(1,128)S(1)}, u32[]{:S(2)}, u32[]{:S(2)}) collective-permute-start(f32[2,9,1,128]{3,2,0,1:T(1,128)S(1)} %pad_maximum_fusion.10), channel_id=1, source_target_pairs={{0,4},{4,8},{8,12},{12,16},{16,20},{20,24},{24,28},{1,5},{5,9},{9,... | collective-permute-start | bytes 27656 | tf_op jit(solution)/shard_map/ppermute | solution.py:15
  11.2 0.9 copy-start
  12.2 5.6 %collective-permute-start.2 = (f32[3,8,1,128]{3,2,1,0:T(1,128)S(1)}, f32[3,8,1,128]{3,2,1,0:T(1,128)S(1)}, u32[]{:S(2)}, u32[]{:S(2)}) collective-permute-start(f32[3,8,1,128]{3,2,1,0:T(1,128)S(1)} %get-tuple-element.379), channel_id=1, source_target_pairs={{0,4},{4,8},{8,12},{12,16},{16,20},{20,24},{24,28},{1,5},{5,9},{9,... | collective-permute-start | bytes 36872 | tf_op jit(solution)/shard_map/ppermute | solution.py:23
  16.4 6.0 %collective-permute-start.3 = (f32[3,8,1,128]{3,2,1,0:T(1,128)S(1)}, f32[3,8,1,128]{3,2,1,0:T(1,128)S(1)}, u32[]{:S(2)}, u32[]{:S(2)}) collective-permute-start(f32[3,8,1,128]{3,2,1,0:T(1,128)S(1)} %get-tuple-element.380), channel_id=1, source_target_pairs={{4,0},{8,4},{12,8},{16,12},{20,16},{24,20},{28,24},{5,1},{9,5},{13... | collective-permute-start | bytes 36872 | tf_op jit(solution)/shard_map/ppermute | solution.py:26
  22.4 2.7 %copy-start.1 = (f32[24,24]{1,0:T(8,128)S(1)}, f32[24,24]{1,0:T(8,128)}, u32[]{:S(2)}) copy-start(f32[24,24]{1,0:T(8,128)} %param.17) | copy-start | bytes 6916
  22.4 2.7 %copy-start.2 = (f32[24,24]{1,0:T(8,128)S(1)}, f32[24,24]{1,0:T(8,128)}, u32[]{:S(2)}) copy-start(f32[24,24]{1,0:T(8,128)} %param.16) | copy-start | bytes 6916
  22.4 2.8 %collective-permute-start.4 = (f32[3,1,10,128]{3,2,1,0:T(8,128)S(1)}, f32[3,1,10,128]{3,2,1,0:T(8,128)S(1)}, u32[]{:S(2)}, u32[]{:S(2)}) collective-permute-start(f32[3,1,10,128]{3,2,1,0:T(8,128)S(1)} %get-tuple-element.372), channel_id=1, source_target_pairs={{0,1},{1,2},{2,3},{4,5},{5,6},{6,7},{8,9},{9,10},{10,11},{12,13},{... | collective-permute-start | bytes 46088 | tf_op jit(solution)/shard_map/ppermute | solution.py:23
  23.8 7.2 %collective-permute-start.5 = (f32[3,1,10,128]{3,2,1,0:T(8,128)S(1)}, f32[3,1,10,128]{3,2,1,0:T(8,128)S(1)}, u32[]{:S(2)}, u32[]{:S(2)}) collective-permute-start(f32[3,1,10,128]{3,2,1,0:T(8,128)S(1)} %get-tuple-element.371), channel_id=1, source_target_pairs={{1,0},{2,1},{3,2},{5,4},{6,5},{7,6},{9,8},{10,9},{11,10},{13,12},{... | collective-permute-start | bytes 46088 | tf_op jit(solution)/shard_map/ppermute | solution.py:26
  85.5 5.6 %collective-permute-start.6 = (f32[3,8,1,128]{3,2,1,0:T(1,128)S(1)}, f32[3,8,1,128]{3,2,1,0:T(1,128)S(1)}, u32[]{:S(2)}, u32[]{:S(2)}) collective-permute-start(f32[3,8,1,128]{3,2,1,0:T(1,128)S(1)} %get-tuple-element.377), channel_id=1, source_target_pairs={{0,4},{4,8},{8,12},{12,16},{16,20},{20,24},{24,28},{1,5},{5,9},{9,... | collective-permute-start | bytes 36872 | tf_op jit(solution)/shard_map/ppermute | solution.py:23
  89.6 5.6 %collective-permute-start.7 = (f32[3,8,1,128]{3,2,1,0:T(1,128)S(1)}, f32[3,8,1,128]{3,2,1,0:T(1,128)S(1)}, u32[]{:S(2)}, u32[]{:S(2)}) collective-permute-start(f32[3,8,1,128]{3,2,1,0:T(1,128)S(1)} %get-tuple-element.378), channel_id=1, source_target_pairs={{4,0},{8,4},{12,8},{16,12},{20,16},{24,20},{28,24},{5,1},{9,5},{13... | collective-permute-start | bytes 36872 | tf_op jit(solution)/shard_map/ppermute | solution.py:26
  95.2 2.6 %collective-permute-start.8 = (f32[3,1,10,128]{3,2,1,0:T(8,128)S(1)}, f32[3,1,10,128]{3,2,1,0:T(8,128)S(1)}, u32[]{:S(2)}, u32[]{:S(2)}) collective-permute-start(f32[3,1,10,128]{3,2,1,0:T(8,128)S(1)} %get-tuple-element.368), channel_id=1, source_target_pairs={{0,1},{1,2},{2,3},{4,5},{5,6},{6,7},{8,9},{9,10},{10,11},{12,13},{... | collective-permute-start | bytes 46088 | tf_op jit(solution)/shard_map/ppermute | solution.py:23
  96.5 3.5 %collective-permute-start.9 = (f32[3,1,10,128]{3,2,1,0:T(8,128)S(1)}, f32[3,1,10,128]{3,2,1,0:T(8,128)S(1)}, u32[]{:S(2)}, u32[]{:S(2)}) collective-permute-start(f32[3,1,10,128]{3,2,1,0:T(8,128)S(1)} %get-tuple-element.367), channel_id=1, source_target_pairs={{1,0},{2,1},{3,2},{5,4},{6,5},{7,6},{9,8},{10,9},{11,10},{13,12},{... | collective-permute-start | bytes 46088 | tf_op jit(solution)/shard_map/ppermute | solution.py:26
  157.4 5.6 %collective-permute-start.10 = (f32[3,8,1,128]{3,2,1,0:T(1,128)S(1)}, f32[3,8,1,128]{3,2,1,0:T(1,128)S(1)}, u32[]{:S(2)}, u32[]{:S(2)}) collective-permute-start(f32[3,8,1,128]{3,2,1,0:T(1,128)S(1)} %get-tuple-element.375), channel_id=1, source_target_pairs={{0,4},{4,8},{8,12},{12,16},{16,20},{20,24},{24,28},{1,5},{5,9},{9,... | collective-permute-start | bytes 36872 | tf_op jit(solution)/shard_map/ppermute | solution.py:23
  161.6 5.6 %collective-permute-start.11 = (f32[3,8,1,128]{3,2,1,0:T(1,128)S(1)}, f32[3,8,1,128]{3,2,1,0:T(1,128)S(1)}, u32[]{:S(2)}, u32[]{:S(2)}) collective-permute-start(f32[3,8,1,128]{3,2,1,0:T(1,128)S(1)} %get-tuple-element.376), channel_id=1, source_target_pairs={{4,0},{8,4},{12,8},{16,12},{20,16},{24,20},{28,24},{5,1},{9,5},{13... | collective-permute-start | bytes 36872 | tf_op jit(solution)/shard_map/ppermute | solution.py:26
  167.2 2.6 %collective-permute-start.12 = (f32[3,1,10,128]{3,2,1,0:T(8,128)S(1)}, f32[3,1,10,128]{3,2,1,0:T(8,128)S(1)}, u32[]{:S(2)}, u32[]{:S(2)}) collective-permute-start(f32[3,1,10,128]{3,2,1,0:T(8,128)S(1)} %get-tuple-element.364), channel_id=1, source_target_pairs={{0,1},{1,2},{2,3},{4,5},{5,6},{6,7},{8,9},{9,10},{10,11},{12,13},{... | collective-permute-start | bytes 46088 | tf_op jit(solution)/shard_map/ppermute | solution.py:23
  168.5 3.6 %collective-permute-start.13 = (f32[3,1,10,128]{3,2,1,0:T(8,128)S(1)}, f32[3,1,10,128]{3,2,1,0:T(8,128)S(1)}, u32[]{:S(2)}, u32[]{:S(2)}) collective-permute-start(f32[3,1,10,128]{3,2,1,0:T(8,128)S(1)} %get-tuple-element.363), channel_id=1, source_target_pairs={{1,0},{2,1},{3,2},{5,4},{6,5},{7,6},{9,8},{10,9},{11,10},{13,12},{... | collective-permute-start | bytes 46088 | tf_op jit(solution)/shard_map/ppermute | solution.py:26
where the time goes:
time: 231 us; the launch traced here: 229 us
  blocking collectives  129 us (56%)
  starting transfers between devices  30.9 us (13%)
  waiting for transfers between devices  25.7 us (11%)
  local copies, waits for them, and re-layouts  12.1 us (5%)
  between operations  10.5 us (5%)
  other arithmetic  9.69 us (4%)
  matrix products  7.21 us (3%)
  loops' own time  4.67 us (2%)
    psum x3, blocking collectives, inner_sums(): lax.psum((jnp.sum(residual * residual), jnp.sum(residual * image)), ('cur...  129 us
    ppermute x6, waiting for transfers between devices, padded(): lax.ppermute(lax.slice_in_dim(block, 0, width, axis=dim), axis, backward)  23.3 us
    ppermute x6, starting transfers between devices, padded(): lax.ppermute(lax.slice_in_dim(block, block.shape[dim] - width, None, axis...  16.5 us
    ppermute x6, starting transfers between devices, padded(): lax.ppermute(lax.slice_in_dim(block, 0, width, axis=dim), axis, backward)  7.75 us
    dot_general x27, matrix products, layer(): jnp.dot(k_both, scaled, precision=lax.Precision.HIGHEST, preferred_elemen...  7.21 us
    ppermute x2, starting transfers between devices, shifted(): return lax.ppermute(value, axis, pairs)  6.61 us
    another operation x3, loops' own time, node_forces(): _, emitted = lax.scan(layer, start, (lower, upper, layer_coef))  4.67 us
  transfers between devices with their start and end apart: 14, of which 11 were waited for; matrix products, arithmetic and copies ran while one was open for 0% of the time, Pallas kernels for 0%

commit v1 on v0

--- a/solution.py
+++ b/solution.py
@@ -7,6 +7,11 @@
 MATERIALS = 4
 ITERS = 3
 ground_spring = 0.5
+
+
+def register_sums_all(xin):
+    y = jax.lax.psum(xin, "sub")
+    return jax.lax.psum(y, "curve")
 
 
 def shifted(value, axis, by):
@@ -110,7 +115,7 @@
 
 
 def inner_sums(residual, image):
-    return lax.psum((jnp.sum(residual * residual), jnp.sum(residual * image)), ("curve", "sub"))
+    return register_sums_all((jnp.sum(residual * residual), jnp.sum(residual * image)))
 
 
 def local(load, plastic, tile_material, moduli, k_vol, k_dev):

time: 231 us -> 185 us (0.80)
  blocking collectives: 129 us -> 85.6 us
  starting transfers between devices: 30.9 us -> 26 us
  waiting for transfers between devices: 25.7 us -> 28.4 us
    psum x3 -> x6, blocking collectives: 129 us -> 85.6 us  [the longest x3 59.1 us: register_sums_all(): return jax.lax.psum(y, 'curve')]
    ppermute x6, starting transfers between devices: 16.5 us -> 11.6 us  [padded(): lax.ppermute(lax.slice_in_dim(block, block.shape[dim] - width, None, axis...]
    ppermute x6, waiting for transfers between devices: 23.3 us -> 26.1 us  [padded(): lax.ppermute(lax.slice_in_dim(block, 0, width, axis=dim), axis, backward)]
where the time goes in v1:
time: 185 us; the launch traced here: 184 us
  blocking collectives  85.6 us (46%)
  waiting for transfers between devices  28.4 us (15%)
  starting transfers between devices  26 us (14%)
  local copies, waits for them, and re-layouts  12.1 us (7%)
  between operations  10.6 us (6%)
  other arithmetic  9.67 us (5%)
  matrix products  7.21 us (4%)
  loops' own time  4.67 us (3%)
    psum x3, blocking collectives, register_sums_all(): return jax.lax.psum(y, 'curve')  59.1 us
    psum x3, blocking collectives, register_sums_all(): y = jax.lax.psum(xin, 'sub')  26.5 us
    ppermute x6, waiting for transfers between devices, padded(): lax.ppermute(lax.slice_in_dim(block, 0, width, axis=dim), axis, backward)  26.1 us
    ppermute x6, starting transfers between devices, padded(): lax.ppermute(lax.slice_in_dim(block, block.shape[dim] - width, None, axis...  11.6 us
    ppermute x6, starting transfers between devices, padded(): lax.ppermute(lax.slice_in_dim(block, 0, width, axis=dim), axis, backward)  7.75 us
    dot_general x27, matrix products, layer(): jnp.dot(k_both, scaled, precision=lax.Precision.HIGHEST, preferred_elemen...  7.21 us
    ppermute x2, starting transfers between devices, shifted(): return lax.ppermute(value, axis, pairs)  6.61 us
    another operation x3, loops' own time, node_forces(): _, emitted = lax.scan(layer, start, (lower, upper, layer_coef))  4.67 us
  transfers between devices with their start and end apart: 14, of which 11 were waited for; matrix products, arithmetic and copies ran while one was open for 0% of the time, Pallas kernels for 0%

profile of v1, /device:TPU:0, one launch (start us, length us, event | category | flops | bytes accessed | tf_op | source)
XLA Modules:
  0.0 184.2 jit_solution(10038840336318845124)
XLA Ops:
  0.7 0.6 copy-done.3
  1.6 0.8 multiply_bitcast_fusion
  2.4 2.4 %collective-permute-start = (f32[2,1,8,128]{3,2,0,1:T(8,128)S(1)}, f32[2,1,8,128]{3,2,0,1:T(8,128)S(1)}, u32[]{:S(2)}, u32[]{:S(2)}) collective-permute-start(f32[2,1,8,128]{3,2,0,1:T(8,128)S(1)} %pad_maximum_fusion.12), channel_id=1, source_target_pairs={{0,1},{1,2},{2,3},{4,5},{5,6},{6,7},{8,9},{9,10},{10,11},{12,13},{... | collective-permute-start | bytes 24584 | tf_op jit(solution)/shard_map/ppermute | solution.py:20
  4.8 0.7 collective-permute-done
  5.6 4.2 %collective-permute-start.1 = (f32[2,9,1,128]{3,2,0,1:T(1,128)S(1)}, f32[2,9,1,128]{3,2,0,1:T(1,128)S(1)}, u32[]{:S(2)}, u32[]{:S(2)}) collective-permute-start(f32[2,9,1,128]{3,2,0,1:T(1,128)S(1)} %pad_maximum_fusion.10), channel_id=1, source_target_pairs={{0,4},{4,8},{8,12},{12,16},{16,20},{20,24},{24,28},{1,5},{5,9},{9,... | collective-permute-start | bytes 27656 | tf_op jit(solution)/shard_map/ppermute | solution.py:20
  9.8 1.3 collective-permute-done.1
  11.4 0.8 copy-done
  12.2 4.2 %collective-permute-start.2 = (f32[3,8,1,128]{3,2,1,0:T(1,128)S(1)}, f32[3,8,1,128]{3,2,1,0:T(1,128)S(1)}, u32[]{:S(2)}, u32[]{:S(2)}) collective-permute-start(f32[3,8,1,128]{3,2,1,0:T(1,128)S(1)} %get-tuple-element.385), channel_id=1, source_target_pairs={{0,4},{4,8},{8,12},{12,16},{16,20},{20,24},{24,28},{1,5},{5,9},{9,... | collective-permute-start | bytes 36872 | tf_op jit(solution)/shard_map/ppermute | solution.py:28
  16.4 1.3 collective-permute-start.3
  17.7 4.6 %collective-permute-done.3 = f32[3,8,1,128]{3,2,1,0:T(1,128)S(1)} collective-permute-done((f32[3,8,1,128]{3,2,1,0:T(1,128)S(1)}, f32[3,8,1,128]{3,2,1,0:T(1,128)S(1)}, u32[]{:S(2)}, u32[]{:S(2)}) %collective-permute-start.3) | collective-permute-done | bytes 12320 | tf_op jit(solution)/shard_map/ppermute | solution.py:31
  22.4 1.4 collective-permute-start.4
  23.8 1.3 collective-permute-start.5
  25.2 5.8 %collective-permute-done.5 = f32[3,1,10,128]{3,2,1,0:T(8,128)S(1)} collective-permute-done((f32[3,1,10,128]{3,2,1,0:T(8,128)S(1)}, f32[3,1,10,128]{3,2,1,0:T(8,128)S(1)}, u32[]{:S(2)}, u32[]{:S(2)}) %collective-permute-start.5) | collective-permute-done | bytes 15392 | tf_op jit(solution)/shard_map/ppermute | solution.py:31
  31.0 9.3 %while.39 = (s32[]{:T(128)}, f32[3,8,128]{2,1,0:T(8,128)S(1)}, f32[9,3,8,128]{3,2,0,1:T(8,128)S(1)}, f32[9,2,9,128]{3,2,1,0:T(8,128)S(1)}, f32[9,3,10,128]{3,2,0...) while((s32[]{:T(128)}, f32[3,8,128]{2,1,0:T(8,128)S(1)}, ...), condition=%wide.region_5.6_spmd.clone, body=%wide.region_4.5_spmd.clone.sunk | while | flops 16060420 | bytes 1924459 | solution.py:113
  31.4 0.3 convolution_bitcast_fusion.6
  32.4 0.3 convolution_bitcast_fusion.6
  33.5 0.3 convolution_bitcast_fusion.6
  34.5 0.3 convolution_bitcast_fusion.6
  35.5 0.3 convolution_bitcast_fusion.6
  37.6 0.3 convolution_bitcast_fusion.6
  38.6 0.3 convolution_bitcast_fusion.6
  39.6 0.3 convolution_bitcast_fusion.6
  40.3 0.6 multiply_reduce_fusion.4
  40.9 8.8 %all-reduce.33 = (f32[]{:T(128)}, f32[]{:T(128)}) all-reduce(f32[]{:T(128)} %get-tuple-element.256, f32[]{:T(128)} %get-tuple-element.255), channel_id=1, replica_groups=mesh['curve'=8,'sub'=4] {'sub'}, use_global_device_ids=true, to_apply=%region_2.3 | all-reduce | flops 2 | bytes 16 | tf_op jit(solution)/shard_map/psum | solution.py:13
  49.8 20.9 %all-reduce.30 = (f32[]{:T(128)}, f32[]{:T(128)}) all-reduce(f32[]{:T(128)} %get-tuple-element.309, f32[]{:T(128)} %get-tuple-element.310), channel_id=1, replica_groups=mesh['curve'=8,'sub'=4] {'curve'}, use_global_device_ids=true, to_apply=%region_3.4 | all-reduce | flops 2 | bytes 16 | tf_op jit(solution)/shard_map/psum | solution.py:14
  72.0 1.3 collective-permute-start.6
  73.3 1.3 collective-permute-start.7
  74.7 4.2 %collective-permute-done.7 = f32[3,8,1,128]{3,2,1,0:T(1,128)S(1)} collective-permute-done((f32[3,8,1,128]{3,2,1,0:T(1,128)S(1)}, f32[3,8,1,128]{3,2,1,0:T(1,128)S(1)}, u32[]{:S(2)}, u32[]{:S(2)}) %collective-permute-start.7) | collective-permute-done | bytes 12320 | tf_op jit(solution)/shard_map/ppermute | solution.py:31
  78.9 1.3 collective-permute-start.8
  80.2 1.3 collective-permute-start.9
  81.6 3.6 %collective-permute-done.9 = f32[3,1,10,128]{3,2,1,0:T(8,128)S(1)} collective-permute-done((f32[3,1,10,128]{3,2,1,0:T(8,128)S(1)}, f32[3,1,10,128]{3,2,1,0:T(8,128)S(1)}, u32[]{:S(2)}, u32[]{:S(2)}) %collective-permute-start.9) | collective-permute-done | bytes 15392 | tf_op jit(solution)/shard_map/ppermute | solution.py:31
  85.3 9.3 %while.40 = (s32[]{:T(128)}, f32[3,8,128]{2,1,0:T(8,128)S(1)}, f32[9,3,8,128]{3,2,0,1:T(8,128)S(1)}, f32[9,2,9,128]{3,2,1,0:T(8,128)S(1)}, f32[9,3,10,128]{3,2,0...) while((s32[]{:T(128)}, f32[3,8,128]{2,1,0:T(8,128)S(1)}, ...), condition=%wide.region_13.14_spmd.clone, body=%wide.region_12.13_spmd.clone.sunk | while | flops 16060420 | bytes 1924459 | solution.py:113
  85.6 0.3 convolution_bitcast_fusion.7
  86.7 0.3 convolution_bitcast_fusion.7
  87.7 0.3 convolution_bitcast_fusion.7
  88.7 0.3 convolution_bitcast_fusion.7
  89.7 0.3 convolution_bitcast_fusion.7
  90.8 0.3 convolution_bitcast_fusion.7
  91.8 0.3 convolution_bitcast_fusion.7
  92.8 0.3 convolution_bitcast_fusion.7
  93.8 0.3 convolution_bitcast_fusion.7
  94.5 0.7 multiply_reduce_fusion.2
  95.2 8.9 %all-reduce.32 = (f32[]{:T(128)}, f32[]{:T(128)}) all-reduce(f32[]{:T(128)} %get-tuple-element.254, f32[]{:T(128)} %get-tuple-element.253), channel_id=1, replica_groups=mesh['curve'=8,'sub'=4] {'sub'}, use_global_device_ids=true, to_apply=%region_10.11 | all-reduce | flops 2 | bytes 16 | tf_op jit(solution)/shard_map/psum | solution.py:13
  104.1 19.5 %all-reduce.29 = (f32[]{:T(128)}, f32[]{:T(128)}) all-reduce(f32[]{:T(128)} %get-tuple-element.307, f32[]{:T(128)} %get-tuple-element.308), channel_id=1, replica_groups=mesh['curve'=8,'sub'=4] {'curve'}, use_global_device_ids=true, to_apply=%region_11.12 | all-reduce | flops 2 | bytes 16 | tf_op jit(solution)/shard_map/psum | solution.py:14
  128.2 2.2 %collective-permute-start.10 = (f32[3,8,1,128]{3,2,1,0:T(1,128)S(1)}, f32[3,8,1,128]{3,2,1,0:T(1,128)S(1)}, u32[]{:S(2)}, u32[]{:S(2)}) collective-permute-start(f32[3,8,1,128]{3,2,1,0:T(1,128)S(1)} %get-tuple-element.381), channel_id=1, source_target_pairs={{0,4},{4,8},{8,12},{12,16},{16,20},{20,24},{24,28},{1,5},{5,9},{9,... | collective-permute-start | bytes 36872 | tf_op jit(solution)/shard_map/ppermute | solution.py:28
  130.4 1.3 collective-permute-start.11
  131.7 4.2 %collective-permute-done.11 = f32[3,8,1,128]{3,2,1,0:T(1,128)S(1)} collective-permute-done((f32[3,8,1,128]{3,2,1,0:T(1,128)S(1)}, f32[3,8,1,128]{3,2,1,0:T(1,128)S(1)}, u32[]{:S(2)}, u32[]{:S(2)}) %collective-permute-start.11) | collective-permute-done | bytes 12320 | tf_op jit(solution)/shard_map/ppermute | solution.py:31
  136.0 1.3 collective-permute-start.12
  137.3 1.3 collective-permute-start.13
  138.6 3.6 %collective-permute-done.13 = f32[3,1,10,128]{3,2,1,0:T(8,128)S(1)} collective-permute-done((f32[3,1,10,128]{3,2,1,0:T(8,128)S(1)}, f32[3,1,10,128]{3,2,1,0:T(8,128)S(1)}, u32[]{:S(2)}, u32[]{:S(2)}) %collective-permute-start.13) | collective-permute-done | bytes 15392 | tf_op jit(solution)/shard_map/ppermute | solution.py:31
  142.3 9.3 %while.41 = (s32[]{:T(128)}, f32[3,8,128]{2,1,0:T(8,128)S(1)}, f32[9,3,8,128]{3,2,0,1:T(8,128)S(1)}, f32[9,2,9,128]{3,2,1,0:T(8,128)S(1)}, f32[9,3,10,128]{3,2,0...) while((s32[]{:T(128)}, f32[3,8,128]{2,1,0:T(8,128)S(1)}, ...), condition=%wide.region_21.22_spmd.clone, body=%wide.region_20.21_spmd.clone.sunk | while | flops 16060420 | bytes 1924459 | solution.py:113
  142.7 0.3 convolution_bitcast_fusion.8
  143.7 0.3 convolution_bitcast_fusion.8
  144.7 0.3 convolution_bitcast_fusion.8
  145.7 0.3 convolution_bitcast_fusion.8
  146.8 0.3 convolution_bitcast_fusion.8
  147.8 0.3 convolution_bitcast_fusion.8
  148.8 0.3 convolution_bitcast_fusion.8
  149.8 0.3 convolution_bitcast_fusion.8
  150.9 0.3 convolution_bitcast_fusion.8
  151.6 0.6 multiply_reduce_fusion
  152.2 8.8 %all-reduce.31 = (f32[]{:T(128)}, f32[]{:T(128)}) all-reduce(f32[]{:T(128)} %get-tuple-element.252, f32[]{:T(128)} %get-tuple-element.251), channel_id=1, replica_groups=mesh['curve'=8,'sub'=4] {'sub'}, use_global_device_ids=true, to_apply=%region_18.19 | all-reduce | flops 2 | bytes 16 | tf_op jit(solution)/shard_map/psum | solution.py:13
  161.0 18.7 %all-reduce.28 = (f32[]{:T(128)}, f32[]{:T(128)}) all-reduce(f32[]{:T(128)} %get-tuple-element.305, f32[]{:T(128)} %get-tuple-element.306), channel_id=1, replica_groups=mesh['curve'=8,'sub'=4] {'curve'}, use_global_device_ids=true, to_apply=%region_19.20 | all-reduce | flops 2 | bytes 16 | tf_op jit(solution)/shard_map/psum | solution.py:14
  183.5 0.7 multiply_subtract_fusion
  (804 shorter events, 17.4 us)
Async XLA Ops:
  0.6 0.7 copy-start.3
  0.7 0.7 copy-start.4
  2.4 3.2 %collective-permute-start = (f32[2,1,8,128]{3,2,0,1:T(8,128)S(1)}, f32[2,1,8,128]{3,2,0,1:T(8,128)S(1)}, u32[]{:S(2)}, u32[]{:S(2)}) collective-permute-start(f32[2,1,8,128]{3,2,0,1:T(8,128)S(1)} %pad_maximum_fusion.12), channel_id=1, source_target_pairs={{0,1},{1,2},{2,3},{4,5},{5,6},{6,7},{8,9},{9,10},{10,11},{12,13},{... | collective-permute-start | bytes 24584 | tf_op jit(solution)/shard_map/ppermute | solution.py:20
  5.6 5.6 %collective-permute-start.1 = (f32[2,9,1,128]{3,2,0,1:T(1,128)S(1)}, f32[2,9,1,128]{3,2,0,1:T(1,128)S(1)}, u32[]{:S(2)}, u32[]{:S(2)}) collective-permute-start(f32[2,9,1,128]{3,2,0,1:T(1,128)S(1)} %pad_maximum_fusion.10), channel_id=1, source_target_pairs={{0,4},{4,8},{8,12},{12,16},{16,20},{20,24},{24,28},{1,5},{5,9},{9,... | collective-permute-start | bytes 27656 | tf_op jit(solution)/shard_map/ppermute | solution.py:20
  11.2 0.9 copy-start
  12.2 5.6 %collective-permute-start.2 = (f32[3,8,1,128]{3,2,1,0:T(1,128)S(1)}, f32[3,8,1,128]{3,2,1,0:T(1,128)S(1)}, u32[]{:S(2)}, u32[]{:S(2)}) collective-permute-start(f32[3,8,1,128]{3,2,1,0:T(1,128)S(1)} %get-tuple-element.385), channel_id=1, source_target_pairs={{0,4},{4,8},{8,12},{12,16},{16,20},{20,24},{24,28},{1,5},{5,9},{9,... | collective-permute-start | bytes 36872 | tf_op jit(solution)/shard_map/ppermute | solution.py:28
  16.4 6.0 %collective-permute-start.3 = (f32[3,8,1,128]{3,2,1,0:T(1,128)S(1)}, f32[3,8,1,128]{3,2,1,0:T(1,128)S(1)}, u32[]{:S(2)}, u32[]{:S(2)}) collective-permute-start(f32[3,8,1,128]{3,2,1,0:T(1,128)S(1)} %get-tuple-element.386), channel_id=1, source_target_pairs={{4,0},{8,4},{12,8},{16,12},{20,16},{24,20},{28,24},{5,1},{9,5},{13... | collective-permute-start | bytes 36872 | tf_op jit(solution)/shard_map/ppermute | solution.py:31
  22.4 2.7 %copy-start.1 = (f32[24,24]{1,0:T(8,128)S(1)}, f32[24,24]{1,0:T(8,128)}, u32[]{:S(2)}) copy-start(f32[24,24]{1,0:T(8,128)} %param.17) | copy-start | bytes 6916
  22.4 2.7 %copy-start.2 = (f32[24,24]{1,0:T(8,128)S(1)}, f32[24,24]{1,0:T(8,128)}, u32[]{:S(2)}) copy-start(f32[24,24]{1,0:T(8,128)} %param.16) | copy-start | bytes 6916
  22.4 2.8 %collective-permute-start.4 = (f32[3,1,10,128]{3,2,1,0:T(8,128)S(1)}, f32[3,1,10,128]{3,2,1,0:T(8,128)S(1)}, u32[]{:S(2)}, u32[]{:S(2)}) collective-permute-start(f32[3,1,10,128]{3,2,1,0:T(8,128)S(1)} %get-tuple-element.378), channel_id=1, source_target_pairs={{0,1},{1,2},{2,3},{4,5},{5,6},{6,7},{8,9},{9,10},{10,11},{12,13},{... | collective-permute-start | bytes 46088 | tf_op jit(solution)/shard_map/ppermute | solution.py:28
  23.8 7.2 %collective-permute-start.5 = (f32[3,1,10,128]{3,2,1,0:T(8,128)S(1)}, f32[3,1,10,128]{3,2,1,0:T(8,128)S(1)}, u32[]{:S(2)}, u32[]{:S(2)}) collective-permute-start(f32[3,1,10,128]{3,2,1,0:T(8,128)S(1)} %get-tuple-element.377), channel_id=1, source_target_pairs={{1,0},{2,1},{3,2},{5,4},{6,5},{7,6},{9,8},{10,9},{11,10},{13,12},{... | collective-permute-start | bytes 46088 | tf_op jit(solution)/shard_map/ppermute | solution.py:31
  72.0 2.7 %collective-permute-start.6 = (f32[3,8,1,128]{3,2,1,0:T(1,128)S(1)}, f32[3,8,1,128]{3,2,1,0:T(1,128)S(1)}, u32[]{:S(2)}, u32[]{:S(2)}) collective-permute-start(f32[3,8,1,128]{3,2,1,0:T(1,128)S(1)} %get-tuple-element.383), channel_id=1, source_target_pairs={{0,4},{4,8},{8,12},{12,16},{16,20},{20,24},{24,28},{1,5},{5,9},{9,... | collective-permute-start | bytes 36872 | tf_op jit(solution)/shard_map/ppermute | solution.py:28
  73.3 5.6 %collective-permute-start.7 = (f32[3,8,1,128]{3,2,1,0:T(1,128)S(1)}, f32[3,8,1,128]{3,2,1,0:T(1,128)S(1)}, u32[]{:S(2)}, u32[]{:S(2)}) collective-permute-start(f32[3,8,1,128]{3,2,1,0:T(1,128)S(1)} %get-tuple-element.384), channel_id=1, source_target_pairs={{4,0},{8,4},{12,8},{16,12},{20,16},{24,20},{28,24},{5,1},{9,5},{13... | collective-permute-start | bytes 36872 | tf_op jit(solution)/shard_map/ppermute | solution.py:31
  78.9 2.6 %collective-permute-start.8 = (f32[3,1,10,128]{3,2,1,0:T(8,128)S(1)}, f32[3,1,10,128]{3,2,1,0:T(8,128)S(1)}, u32[]{:S(2)}, u32[]{:S(2)}) collective-permute-start(f32[3,1,10,128]{3,2,1,0:T(8,128)S(1)} %get-tuple-element.374), channel_id=1, source_target_pairs={{0,1},{1,2},{2,3},{4,5},{5,6},{6,7},{8,9},{9,10},{10,11},{12,13},{... | collective-permute-start | bytes 46088 | tf_op jit(solution)/shard_map/ppermute | solution.py:28
  80.2 5.0 %collective-permute-start.9 = (f32[3,1,10,128]{3,2,1,0:T(8,128)S(1)}, f32[3,1,10,128]{3,2,1,0:T(8,128)S(1)}, u32[]{:S(2)}, u32[]{:S(2)}) collective-permute-start(f32[3,1,10,128]{3,2,1,0:T(8,128)S(1)} %get-tuple-element.373), channel_id=1, source_target_pairs={{1,0},{2,1},{3,2},{5,4},{6,5},{7,6},{9,8},{10,9},{11,10},{13,12},{... | collective-permute-start | bytes 46088 | tf_op jit(solution)/shard_map/ppermute | solution.py:31
  128.2 3.6 %collective-permute-start.10 = (f32[3,8,1,128]{3,2,1,0:T(1,128)S(1)}, f32[3,8,1,128]{3,2,1,0:T(1,128)S(1)}, u32[]{:S(2)}, u32[]{:S(2)}) collective-permute-start(f32[3,8,1,128]{3,2,1,0:T(1,128)S(1)} %get-tuple-element.381), channel_id=1, source_target_pairs={{0,4},{4,8},{8,12},{12,16},{16,20},{20,24},{24,28},{1,5},{5,9},{9,... | collective-permute-start | bytes 36872 | tf_op jit(solution)/shard_map/ppermute | solution.py:28
  130.4 5.6 %collective-permute-start.11 = (f32[3,8,1,128]{3,2,1,0:T(1,128)S(1)}, f32[3,8,1,128]{3,2,1,0:T(1,128)S(1)}, u32[]{:S(2)}, u32[]{:S(2)}) collective-permute-start(f32[3,8,1,128]{3,2,1,0:T(1,128)S(1)} %get-tuple-element.382), channel_id=1, source_target_pairs={{4,0},{8,4},{12,8},{16,12},{20,16},{24,20},{28,24},{5,1},{9,5},{13... | collective-permute-start | bytes 36872 | tf_op jit(solution)/shard_map/ppermute | solution.py:31
  136.0 2.6 %collective-permute-start.12 = (f32[3,1,10,128]{3,2,1,0:T(8,128)S(1)}, f32[3,1,10,128]{3,2,1,0:T(8,128)S(1)}, u32[]{:S(2)}, u32[]{:S(2)}) collective-permute-start(f32[3,1,10,128]{3,2,1,0:T(8,128)S(1)} %get-tuple-element.370), channel_id=1, source_target_pairs={{0,1},{1,2},{2,3},{4,5},{5,6},{6,7},{8,9},{9,10},{10,11},{12,13},{... | collective-permute-start | bytes 46088 | tf_op jit(solution)/shard_map/ppermute | solution.py:28
  137.3 5.0 %collective-permute-start.13 = (f32[3,1,10,128]{3,2,1,0:T(8,128)S(1)}, f32[3,1,10,128]{3,2,1,0:T(8,128)S(1)}, u32[]{:S(2)}, u32[]{:S(2)}) collective-permute-start(f32[3,1,10,128]{3,2,1,0:T(8,128)S(1)} %get-tuple-element.369), channel_id=1, source_target_pairs={{1,0},{2,1},{3,2},{5,4},{6,5},{7,6},{9,8},{10,9},{11,10},{13,12},{... | collective-permute-start | bytes 46088 | tf_op jit(solution)/shard_map/ppermute | solution.py:31
